TPU v7x, 32 devices: a whole 2x2x4 slice. The times are simulated.
32 devices in a mesh: freq: 16 (over z, y, core), rows: 2 (over x).
Axes of the slice: x: 2, y: 2, z: 4, core: 2. Of those that a mesh axis runs over, the one named last changes fastest.
Arguments:
- kernel: bfloat16 [2, 128, 2048, 2048], P(None, 'freq', 'rows'), may hold values from -0.25 to 0.25
- tile_mask: int32 [128, 16, 16], P('freq', 'rows'), may hold values 0 or 1
- direct: float32 [2048, 128, 512], P(('rows', 'freq')), may hold values from -6 to 6
- onsets: int32 [2048, 128], P(('rows', 'freq')), may hold values from 64 to 447
Outputs:
- focusing: float32 [2048, 128, 512], P(('rows', 'freq'))
Inputs may be any that keep to these rules, and one draw needn't show every extreme that they name: `tile_mask`: 0 drops a tile, 1 keeps it.
All inputs are finite; a program needn't handle non-finite values. No bound on the sum of `tile_mask` on one device may be relied on, other than what follows from the above.
Results may differ from a plain program's by a relative error of at most 0.0026.
Values may be sent and summed in bfloat16 or wider, within the bound.
No kernel may reach another device: no remote copies, remote signals or barrier semaphores. Data moves between devices by JAX's collectives and lax.ppermute only.
A program may use at most 320 MiB of HBM per device.

v0:
```python
import math
import jax
import jax.numpy as jnp
from jax import lax
from jax.sharding import PartitionSpec as P

NF = 128
NT = 512
TILE = 128
ITERS = 2


def phase_table():
    freq_ids = jnp.arange(NF, dtype=jnp.int32) + 1
    time_ids = jnp.arange(NT, dtype=jnp.int32)
    phase_ids = freq_ids[:, None] * time_ids[None, :] % NT
    angles = phase_ids.astype(jnp.float32) * (2.0 * math.pi / NT)
    norm_scale = math.sqrt(2.0 / NT)
    return jnp.stack([jnp.cos(angles), -jnp.sin(angles)]) * norm_scale


def multiply(weights, fields):
    real_real = jnp.einsum(
        "fmk,fkp->fmp", weights[0], fields[0], preferred_element_type=jnp.float32
    )
    imag_imag = jnp.einsum(
        "fmk,fkp->fmp", weights[1], fields[1], preferred_element_type=jnp.float32
    )
    real_imag = jnp.einsum(
        "fmk,fkp->fmp", weights[0], fields[1], preferred_element_type=jnp.float32
    )
    imag_real = jnp.einsum(
        "fmk,fkp->fmp", weights[1], fields[0], preferred_element_type=jnp.float32
    )
    return jnp.stack([real_real - imag_imag, real_imag + imag_real])


def products(masked, fields):
    return multiply(masked, lax.all_gather(fields, "rows", axis=2, tiled=True))


def forward(masked, fields, direct, window, dft_table):
    bands = products(masked, fields).astype(jnp.bfloat16)
    traces = lax.all_to_all(bands, "freq", split_axis=2, concat_axis=1, tiled=True)
    series = jnp.einsum(
        "kjrp,kjt->rpt", traces.astype(jnp.float32), dft_table, precision=lax.Precision.HIGHEST
    )
    return direct - jnp.where(window, series, 0.0)


def to_bands(focusing, dft_table):
    spectra = jnp.einsum(
        "rpt,kjt->kjrp", focusing, dft_table, precision=lax.Precision.HIGHEST
    ).astype(jnp.bfloat16)
    bands = lax.all_to_all(spectra, "freq", split_axis=1, concat_axis=2, tiled=True)
    return bands


def local(kernel, tile_mask, direct, onsets):
    dft_table = phase_table()
    full_mask = jnp.repeat(jnp.repeat(tile_mask, TILE, axis=1), TILE, axis=2).astype(jnp.bfloat16)
    masked = kernel * full_mask[None]
    time_ids = jnp.arange(NT, dtype=jnp.int32)
    window = time_ids[None, None, :] < onsets[:, :, None]
    fields = to_bands(direct, dft_table)
    focusing = direct
    for iteration in range(ITERS):
        focusing = forward(masked, fields, direct, window, dft_table)
        if iteration + 1 < ITERS:
            fields = to_bands(focusing, dft_table)
    return focusing


def solution(mesh):
    return jax.shard_map(
        local,
        mesh=mesh,
        in_specs=(
            P(None, "freq", "rows", None),
            P("freq", "rows", None),
            P(("rows", "freq"), None, None),
            P(("rows", "freq"), None),
        ),
        out_specs=P(("rows", "freq"), None, None),
        check_vma=False,
    )
```

profile of v0, /device:TPU:1, one launch (start us, length us, event | category | flops | bytes accessed | tf_op | source)
XLA Modules:
  0.0 853.0 jit_solution(786638177936812693)
XLA Ops:
  6.5 1.1 fusion.40
  7.7 0.7 copy-done
  8.4 16.9 %fusion.20 = bf16[2,128,64,128]{3,1,2,0:T(8,128)(2,1)S(1)} fusion(f32[64,128,512]{2,1,0:T(8,128)} %param.6, f32[1,128,512]{2,1,0:T(8,128)S(1)} %get-tuple-element.6, f32[1,128,512]{2,1,0:T(8,128)S(1)} %get-tuple-element.5), kind=kOutput, calls=%fused_computation.35 | convolution fusion | flops 12887261184 | bytes 21495808 | tf_op jit(solution)/shard_map/rpt,kjt->kjrp/dot_general | solution.py:52
  25.4 4.7 copy.21
  30.1 7.3 all-to-all-start
  37.8 21.0 %broadcast_in_dim.17 = bf16[8,1024,16,128]{3,2,1,0:T(8,128)(2,1)} broadcast(bf16[8,1024,16]{2,1,0:T(8,128)(2,1)S(1)} %bitcast.116), dimensions={0,1,2} | broadcast | bytes 33816576 | tf_op jit(solution)/shard_map/broadcast_in_dim | solution.py:61
  58.7 49.3 %convert_element_type.43 = bf16[8,1024,2048]{2,1,0:T(8,128)(2,1)} reshape(bf16[8,1024,16,128]{3,2,1,0:T(8,128)(2,1)} %broadcast_in_dim.17) | data formatting | bytes 67108864 | tf_op jit(solution)/shard_map/convert_element_type | solution.py:61
  108.0 7.5 all-to-all-done
  115.6 5.6 copy.22
  121.4 56.1 %broadcast_multiply_fusion = bf16[2,8,1024,2048]{3,2,1,0:T(8,128)(2,1)} fusion(bf16[2,8,1024,2048]{3,2,1,0:T(8,128)(2,1)} %param.4, bf16[8,1024,2048]{2,1,0:T(8,128)(2,1)} %convert_element_type.43), kind=kLoop, calls=%fused_computation.2 | loop fusion | flops 33554432 | bytes 167772160 | tf_op jit(solution)/shard_map/mul | solution.py:62
  177.6 61.4 %all-gather.3.cloned.1.call-done = bf16[2,8,2048,128]{3,2,1,0:T(8,128)(2,1)} async-done(((bf16[2,8,1024,128]{3,2,1,0:T(8,128)(2,1)}), bf16[2,8,2048,128]{3,2,1,0:T(8,128)(2,1)}) %all-gather.3.cloned.1.call-update) | async-done | bytes 8388624 | tf_op jit(solution)/shard_map/all_gather | solution.py:39
  239.0 17.6 %fusion.2 = f32[8,1024,128]{2,1,0:T(8,128)} fusion(bf16[2,8,1024,2048]{3,2,1,0:T(8,128)(2,1)} %broadcast_multiply_fusion, bf16[2,8,2048,128]{3,2,1,0:T(8,128)(2,1)} %all-gather.3.cloned.1.call-done), kind=kOutput, calls=%fused_computation.5 | convolution fusion | flops 4294967296 | bytes 41943040 | tf_op jit(solution)/shard_map/fmk,fkp->fmp/dot_general | solution.py:29
  256.6 17.7 %fusion.3 = f32[8,1024,128]{2,1,0:T(8,128)} fusion(bf16[2,8,1024,2048]{3,2,1,0:T(8,128)(2,1)} %broadcast_multiply_fusion, bf16[2,8,2048,128]{3,2,1,0:T(8,128)(2,1)} %all-gather.3.cloned.1.call-done), kind=kOutput, calls=%fused_computation.6 | convolution fusion | flops 4294967296 | bytes 41943040 | tf_op jit(solution)/shard_map/fmk,fkp->fmp/dot_general | solution.py:23
  274.2 16.7 %fusion.27 = bf16[1,8,1024,128]{3,2,1,0:T(8,128)(2,1)S(1)} fusion(f32[8,1024,128]{2,1,0:T(8,128)} %fusion.2, bf16[2,8,2048,128]{3,2,1,0:T(8,128)(2,1)} %all-gather.3.cloned.1.call-done, bf16[2,8,1024,2048]{3,2,1,0:T(8,128)(2,1)} %broadcast_multiply_fusion), kind=kOutput, calls=%fused_computation.38 | convolution fusion | flops 4297064448 | bytes 44040192 | tf_op jit(solution)/shard_map/fmk,fkp->fmp/dot_general | solution.py:32
  290.9 16.9 %fusion.26 = bf16[1,8,1024,128]{3,2,1,0:T(8,128)(2,1)S(1)} fusion(f32[8,1024,128]{2,1,0:T(8,128)} %fusion.3, bf16[2,8,2048,128]{3,2,1,0:T(8,128)(2,1)} %all-gather.3.cloned.1.call-done, bf16[2,8,1024,2048]{3,2,1,0:T(8,128)(2,1)} %broadcast_multiply_fusion), kind=kOutput, calls=%fused_computation.37 | convolution fusion | flops 4297064448 | bytes 44040192 | tf_op jit(solution)/shard_map/fmk,fkp->fmp/dot_general | solution.py:26
  308.2 2.7 copy.23
  310.9 99.4 %all_to_all.72 = bf16[2,8,1024,128]{3,1,0,2:T(8,128)(2,1)S(1)} all-to-all(bf16[2,8,1024,128]{3,1,0,2:T(8,128)(2,1)S(1)} %copy.23), channel_id=1, replica_groups=mesh['freq'=16,'rows'=2] {'freq'}, dimensions={2} | all-to-all | bytes 8388608 | tf_op jit(solution)/shard_map/all_to_all | solution.py:44
  410.4 1.1 copy.25
  411.5 17.6 %fusion.18 = f32[64,128,512,1]{2,1,3,0:T(8,128)} fusion(bf16[2,128,64,128]{3,2,1,0:T(8,128)(2,1)S(1)} %bitcast.109, f32[1,128,512]{2,1,0:T(8,128)S(1)} %copy-done.3, f32[1,128,512]{2,1,0:T(8,128)S(1)} %copy-done.1), kind=kOutput, calls=%fused_computation.29 | convolution fusion | flops 12885164032 | bytes 21495808 | tf_op jit(solution)/shard_map/kjrp,kjt->rpt/dot_general | solution.py:45
  429.2 18.9 %fusion.23 = bf16[2,128,64,128]{3,1,2,0:T(8,128)(2,1)S(1)} fusion(f32[64,128,512]{2,1,0:T(8,128)S(1)} %bitcast.108, f32[64,128,512,1]{2,1,3,0:T(8,128)} %fusion.18, s32[64,128]{1,0:T(8,128)S(1)} %copy-done.4, f32[1,128,512]{2,1,0:T(8,128)S(1)} %copy-done.3, f32[1,128,512]{2,1,0:T(8,128)S(1)} %copy-done.1), kind=kOutput, calls=%fused_computation.36 | convolution fusion | flops 12899844096 | bytes 38305792 | tf_op jit(solution)/shard_map/rpt,kjt->kjrp/dot_general | solution.py:52
  448.1 2.7 copy.27
  450.8 97.4 %all_to_all.73 = bf16[2,128,64,128]{3,2,0,1:T(8,128)(2,1)S(1)} all-to-all(bf16[2,128,64,128]{3,2,0,1:T(8,128)(2,1)S(1)} %copy.27), channel_id=1, replica_groups=mesh['freq'=16,'rows'=2] {'freq'}, dimensions={1} | all-to-all | bytes 8388608 | tf_op jit(solution)/shard_map/all_to_all | solution.py:55
  548.3 3.0 copy.28
  551.2 102.6 %all-gather.5.cloned.1.call-done = bf16[2,8,2048,128]{3,2,1,0:T(8,128)(2,1)} async-done(((bf16[2,8,1024,128]{3,2,1,0:T(8,128)(2,1)}), bf16[2,8,2048,128]{3,2,1,0:T(8,128)(2,1)}) %all-gather.5.cloned.1.call-update) | async-done | bytes 8388624 | tf_op jit(solution)/shard_map/all_gather | solution.py:39
  653.8 17.7 %fusion = f32[8,1024,128]{2,1,0:T(8,128)} fusion(bf16[2,8,1024,2048]{3,2,1,0:T(8,128)(2,1)} %broadcast_multiply_fusion, bf16[2,8,2048,128]{3,2,1,0:T(8,128)(2,1)} %all-gather.5.cloned.1.call-done), kind=kOutput, calls=%fused_computation.3 | convolution fusion | flops 4294967296 | bytes 41943040 | tf_op jit(solution)/shard_map/fmk,fkp->fmp/dot_general | solution.py:29
  671.5 17.6 %fusion.1 = f32[8,1024,128]{2,1,0:T(8,128)} fusion(bf16[2,8,1024,2048]{3,2,1,0:T(8,128)(2,1)} %broadcast_multiply_fusion, bf16[2,8,2048,128]{3,2,1,0:T(8,128)(2,1)} %all-gather.5.cloned.1.call-done), kind=kOutput, calls=%fused_computation.4 | convolution fusion | flops 4294967296 | bytes 41943040 | tf_op jit(solution)/shard_map/fmk,fkp->fmp/dot_general | solution.py:23
  689.1 16.7 %fusion.29 = bf16[1,8,1024,128]{3,2,1,0:T(8,128)(2,1)S(1)} fusion(f32[8,1024,128]{2,1,0:T(8,128)} %fusion, bf16[2,8,2048,128]{3,2,1,0:T(8,128)(2,1)} %all-gather.5.cloned.1.call-done, bf16[2,8,1024,2048]{3,2,1,0:T(8,128)(2,1)} %broadcast_multiply_fusion), kind=kOutput, calls=%fused_computation.40 | convolution fusion | flops 4297064448 | bytes 44040192 | tf_op jit(solution)/shard_map/fmk,fkp->fmp/dot_general | solution.py:32
  705.7 16.9 %fusion.28 = bf16[1,8,1024,128]{3,2,1,0:T(8,128)(2,1)S(1)} fusion(f32[8,1024,128]{2,1,0:T(8,128)} %fusion.1, bf16[2,8,2048,128]{3,2,1,0:T(8,128)(2,1)} %all-gather.5.cloned.1.call-done, bf16[2,8,1024,2048]{3,2,1,0:T(8,128)(2,1)} %broadcast_multiply_fusion), kind=kOutput, calls=%fused_computation.39 | convolution fusion | flops 4297064448 | bytes 44040192 | tf_op jit(solution)/shard_map/fmk,fkp->fmp/dot_general | solution.py:26
  723.1 2.7 copy.29
  725.8 98.8 %all_to_all.74 = bf16[2,8,1024,128]{3,1,0,2:T(8,128)(2,1)S(1)} all-to-all(bf16[2,8,1024,128]{3,1,0,2:T(8,128)(2,1)S(1)} %copy.29), channel_id=1, replica_groups=mesh['freq'=16,'rows'=2] {'freq'}, dimensions={2} | all-to-all | bytes 8388608 | tf_op jit(solution)/shard_map/all_to_all | solution.py:44
  824.6 1.1 copy.31
  825.7 20.1 %fusion.8 = f32[64,128,512]{2,1,0:T(8,128)} fusion(f32[64,128,512]{2,1,0:T(8,128)} %param.6, s32[64,128]{1,0:T(8,128)S(1)} %copy-done.4, bf16[2,128,64,128]{3,2,1,0:T(8,128)(2,1)S(1)} %bitcast.115, f32[1,128,512]{2,1,0:T(8,128)S(1)} %copy-done.3, f32[1,128,512]{2,1,0:T(8,128)S(1)} %copy-done.1), kind=kOutput, calls=%fused_computation.12 | convolution fusion | flops 12897746944 | bytes 38305792 | tf_op jit(solution)/shard_map/kjrp,kjt->rpt/dot_general | solution.py:45
  (29 shorter events, 1.5 us)
Async XLA Ops:
  7.6 0.7 copy-start
  7.7 0.8 copy-start.2
  25.4 12.1 %copy-start.5 = (s32[8,8,16]{2,1,0:T(8,128)S(1)}, s32[8,8,16]{2,1,0:T(8,128)}, u32[]{:S(2)}) copy-start(s32[8,8,16]{2,1,0:T(8,128)} %param.5) | copy-start | bytes 12292
  30.1 85.5 %all-to-all-start = ((bf16[2,128,64,128]{3,2,0,1:T(8,128)(2,1)}), bf16[2,128,64,128]{3,2,0,1:T(8,128)(2,1)}, u32[]{:S(2)}, u32[]{:S(2)}) async-start(bf16[2,128,64,128]{3,2,0,1:T(8,128)(2,1)} %copy.21), calls=%async_computation | async-start | bytes 8388608 | tf_op jit(solution)/shard_map/all_to_all | solution.py:55
  37.4 201.6 %all-gather.3.cloned.1.call-start = ((), (), s32[]{:S(2)}) async-start(), calls=%async_computation.4 | async-start | bytes 12582912 | tf_op jit(solution)/shard_map/all_gather | solution.py:39
  121.2 532.7 %all-gather.5.cloned.1.call-start = ((), (), s32[]{:S(2)}) async-start(), calls=%async_computation.5 | async-start | bytes 12582912 | tf_op jit(solution)/shard_map/all_gather | solution.py:39
  310.9 100.5 %copy-start.1 = (f32[1,128,512]{2,1,0:T(8,128)S(1)}, f32[1,128,512]{2,1,0:T(8,128)}, u32[]{:S(2)}) copy-start(f32[1,128,512]{2,1,0:T(8,128)} %copy-done) | copy-start | bytes 786436
  310.9 100.5 %copy-start.3 = (f32[1,128,512]{2,1,0:T(8,128)S(1)}, f32[1,128,512]{2,1,0:T(8,128)}, u32[]{:S(2)}) copy-start(f32[1,128,512]{2,1,0:T(8,128)} %copy-done.2) | copy-start | bytes 786436
  410.4 18.8 %slice-start = ((s8[16777216]{0:T(1024)(128)(4,1)}), s8[4194304]{0:T(1024)(128)(4,1)S(1)}, s32[]{:S(2)}) async-start(s8[16777216]{0:T(1024)(128)(4,1)} %bitcast.107), calls=%async_computation.6 | async-start | bytes 8388608
  411.5 17.7 %slice-start.1 = ((s8[16777216]{0:T(1024)(128)(4,1)}), s8[4194304]{0:T(1024)(128)(4,1)S(1)}, s32[]{:S(2)}) async-start(s8[16777216]{0:T(1024)(128)(4,1)} %bitcast.107), calls=%async_computation.7 | async-start | bytes 8388608
  411.5 17.7 %slice-start.2 = ((s8[16777216]{0:T(1024)(128)(4,1)}), s8[4194304]{0:T(1024)(128)(4,1)S(1)}, s32[]{:S(2)}) async-start(s8[16777216]{0:T(1024)(128)(4,1)} %bitcast.107), calls=%async_computation.8 | async-start | bytes 8388608
  411.5 17.7 %slice-start.3 = ((s8[16777216]{0:T(1024)(128)(4,1)}), s8[4194304]{0:T(1024)(128)(4,1)S(1)}, s32[]{:S(2)}) async-start(s8[16777216]{0:T(1024)(128)(4,1)} %bitcast.107), calls=%async_computation.9 | async-start | bytes 8388608
  411.5 17.7 %copy-start.4 = (s32[64,128]{1,0:T(8,128)S(1)}, s32[64,128]{1,0:T(8,128)}, u32[]{:S(2)}) copy-start(s32[64,128]{1,0:T(8,128)} %param.7) | copy-start | bytes 98308
Sparse Core Ops, SparseCore 0:
  121.3 117.6 all-gather.2
  551.4 102.4 all-gather.4
where the time goes:
time: 862 us; the launch traced here: 853 us
  blocking collectives  296 us (34%)
  matrix products  211 us (24%)
  waiting for transfers between devices  172 us (20%)
  local copies, waits for them, and re-layouts  94.9 us (11%)
  other arithmetic  58 us (7%)
  between operations  14.1 us (2%)
    all_to_all x2, blocking collectives, forward(): lax.all_to_all(bands, 'freq', split_axis=2, concat_axis=1, tiled=True)  198 us
    all_gather x2, waiting for transfers between devices, products(): return multiply(masked, lax.all_gather(fields, 'rows', axis=2, tiled=True))  164 us
    all_to_all x1, blocking collectives, to_bands(): lax.all_to_all(spectra, 'freq', split_axis=1, concat_axis=2, tiled=True)  97.4 us
    mul x1, other arithmetic, local(): masked = kernel * full_mask[None]  56.1 us
    convert_element_type x1, local copies, waits for them, and re-layouts, local(): jnp.repeat(jnp.repeat(tile_mask, TILE, axis=1), TILE, axis=2)  49.3 us
    dot_general x2, matrix products, forward(): jnp.einsum('kjrp,kjt->rpt', traces.astype(jnp.float32), dft_table, precis...  37.7 us
    dot_general x2, matrix products, to_bands(): jnp.einsum('rpt,kjt->kjrp', focusing, dft_table, precision=lax.Precision....  35.8 us
    dot_general x2, matrix products, multiply(): jnp.einsum('fmk,fkp->fmp', weights[0], fields[1], preferred_element_type=...  35.2 us
  transfers between devices with their start and end apart: 3, of which 3 were waited for; matrix products, arithmetic and copies ran while one was open for 15% of the time, Pallas kernels for 0%

commit v1 on v0

--- a/solution.py
+++ b/solution.py
@@ -8,6 +8,18 @@
 NT = 512
 TILE = 128
 ITERS = 2
+
+
+def sent_to_each(shard, axis, split, join):
+    ways, here = (lax.axis_size(axis), lax.axis_index(axis))
+    width = shard.shape[split] // ways
+    turned = jnp.roll(shard, -here * width, axis=split)
+    got = [lax.slice_in_dim(turned, 0, width, axis=split)]
+    for far in range(1, ways):
+        sent = lax.slice_in_dim(turned, far * width, (far + 1) * width, axis=split)
+        got.append(lax.ppermute(sent, axis, [(d, (d + far) % ways) for d in range(ways)]))
+    line = jnp.concatenate(got[::-1], axis=join)
+    return jnp.roll(line, (here + 1) * got[0].shape[join], axis=join)
 
 
 def phase_table():
@@ -52,7 +64,7 @@
     spectra = jnp.einsum(
         "rpt,kjt->kjrp", focusing, dft_table, precision=lax.Precision.HIGHEST
     ).astype(jnp.bfloat16)
-    bands = lax.all_to_all(spectra, "freq", split_axis=1, concat_axis=2, tiled=True)
+    bands = sent_to_each(spectra, "freq", 1, 2)
     return bands
 
 

time: 862 us -> 969 us (1.12)
  blocking collectives: 296 us -> 198 us
  waiting for transfers between devices: 172 us -> 267 us
  starting transfers between devices: 7.63 us -> 67.4 us
  other arithmetic: 58 us -> 97.6 us
    ppermute x0 -> x30, waiting for transfers between devices: none -> 105 us  [sent_to_each(): lax.ppermute(sent, axis, [(d, (d + far) % ways) for d in range(ways)])]
    all_to_all x1 -> x0, blocking collectives: 97.4 us -> none  [to_bands(): lax.all_to_all(spectra, 'freq', split_axis=1, concat_axis=2, tiled=True)]
    ppermute x0 -> x30, starting transfers between devices: none -> 67.1 us  [sent_to_each(): lax.ppermute(sent, axis, [(d, (d + far) % ways) for d in range(ways)])]
    concatenate x0 -> x4, other arithmetic: none -> 36.5 us  [the longest x2 32.1 us: sent_to_each(): return jnp.roll(line, (here + 1) * got[0].shape[join], axis=join)]
    squeeze x0 -> x2, local copies, waits for them, and re-layouts: none -> 11.9 us  [multiply(): fields[0]]
  transfers between devices with their start and end apart: 3 -> 32, of which waited for: 3 -> 13; matrix products, arithmetic and copies ran while one was open for 15% -> 14% of each run, Pallas kernels for 0% -> 0%
where the time goes in v1:
time: 969 us; the launch traced here: 960 us
  waiting for transfers between devices  267 us (28%)
  matrix products  215 us (22%)
  blocking collectives  198 us (20%)
  local copies, waits for them, and re-layouts  102 us (11%)
  other arithmetic  97.6 us (10%)
  starting transfers between devices  67.4 us (7%)
  between operations  14.2 us (1%)
    all_to_all x2, blocking collectives, forward(): lax.all_to_all(bands, 'freq', split_axis=2, concat_axis=1, tiled=True)  198 us
    all_gather x2, waiting for transfers between devices, products(): return multiply(masked, lax.all_gather(fields, 'rows', axis=2, tiled=True))  162 us
    ppermute x30, waiting for transfers between devices, sent_to_each(): lax.ppermute(sent, axis, [(d, (d + far) % ways) for d in range(ways)])  105 us
    ppermute x30, starting transfers between devices, sent_to_each(): lax.ppermute(sent, axis, [(d, (d + far) % ways) for d in range(ways)])  67.1 us
    mul x1, other arithmetic, local(): masked = kernel * full_mask[None]  56 us
    convert_element_type x1, local copies, waits for them, and re-layouts, local(): jnp.repeat(jnp.repeat(tile_mask, TILE, axis=1), TILE, axis=2)  49.3 us
    dot_general x2, matrix products, forward(): jnp.einsum('kjrp,kjt->rpt', traces.astype(jnp.float32), dft_table, precis...  37.7 us
    dot_general x2, matrix products, to_bands(): jnp.einsum('rpt,kjt->kjrp', focusing, dft_table, precision=lax.Precision....  36 us
  transfers between devices with their start and end apart: 32, of which 13 were waited for; matrix products, arithmetic and copies ran while one was open for 14% of the time, Pallas kernels for 0%

profile of v1, /device:TPU:1, one launch (start us, length us, event | category | flops | bytes accessed | tf_op | source)
XLA Modules:
  0.0 960.1 jit_solution(2553814570183866566)
XLA Ops:
  7.7 17.1 %fusion.32 = bf16[2,128,64,128]{3,1,2,0:T(8,128)(2,1)S(1)} fusion(f32[64,128,512]{2,1,0:T(8,128)} %param.10, f32[1,128,512]{2,1,0:T(8,128)S(1)} %get-tuple-element.42, f32[1,128,512]{2,1,0:T(8,128)S(1)} %get-tuple-element.41), kind=kOutput, calls=%fused_computation.55 | convolution fusion | flops 12887261184 | bytes 21495808 | tf_op jit(solution)/shard_map/rpt,kjt->kjrp/dot_general | solution.py:64
  31.0 5.8 collective-permute-start.1
  38.4 20.9 %broadcast_in_dim.17 = bf16[8,1024,16,128]{3,2,1,0:T(8,128)(2,1)} broadcast(bf16[8,1024,16]{2,1,0:T(8,128)(2,1)S(1)} %bitcast.89), dimensions={0,1,2} | broadcast | bytes 33816576 | tf_op jit(solution)/shard_map/broadcast_in_dim | solution.py:73
  59.4 49.3 %convert_element_type.43 = bf16[8,1024,2048]{2,1,0:T(8,128)(2,1)} reshape(bf16[8,1024,16,128]{3,2,1,0:T(8,128)(2,1)} %broadcast_in_dim.17) | data formatting | bytes 67108864 | tf_op jit(solution)/shard_map/convert_element_type | solution.py:73
  121.5 4.8 collective-permute-start.10
  126.3 32.0 %collective-permute-done.6 = bf16[2,8,64,128]{3,1,2,0:T(8,128)(2,1)S(1)} collective-permute-done((bf16[2,8,64,128]{3,1,2,0:T(8,128)(2,1)S(1)}, bf16[2,8,64,128]{3,1,2,0:T(8,128)(2,1)S(1)}, u32[]{:S(2)}, u32[]{:S(2)}) %collective-permute-start.6) | collective-permute-done | bytes 262176 | tf_op jit(solution)/shard_map/ppermute | solution.py:20
  158.4 9.3 collective-permute-done.7
  169.8 13.2 %collective-permute-done.9 = bf16[2,8,64,128]{3,1,2,0:T(8,128)(2,1)S(1)} collective-permute-done((bf16[2,8,64,128]{3,1,2,0:T(8,128)(2,1)S(1)}, bf16[2,8,64,128]{3,1,2,0:T(8,128)(2,1)S(1)}, u32[]{:S(2)}, u32[]{:S(2)}) %collective-permute-start.9) | collective-permute-done | bytes 262176 | tf_op jit(solution)/shard_map/ppermute | solution.py:20
  187.5 15.9 %fusion.19 = bf16[2,8,1024,128]{3,1,2,0:T(8,128)(2,1)} fusion(s32[]{:T(128)S(6)} %select_n.53, bf16[2,8,1024,128]{3,1,2,0:T(8,128)(2,1)S(1)} %slice_dynamic-update-slice_fusion.1), kind=kLoop, calls=%fused_computation.32 | loop fusion | flops 2097152 | bytes 8388612 | tf_op jit(solution)/shard_map/jit(_roll_dynamic)/concatenate | solution.py:22
  203.7 56.0 %broadcast_multiply_fusion = bf16[2,8,1024,2048]{3,2,1,0:T(8,128)(2,1)} fusion(bf16[2,8,1024,2048]{3,2,1,0:T(8,128)(2,1)} %param.8, bf16[8,1024,2048]{2,1,0:T(8,128)(2,1)} %convert_element_type.43), kind=kLoop, calls=%fused_computation.2 | loop fusion | flops 33554432 | bytes 167772160 | tf_op jit(solution)/shard_map/mul | solution.py:74
  259.7 51.0 %all-gather.3.cloned.1.call-done = bf16[2,8,2048,128]{3,1,2,0:T(8,128)(2,1)} async-done(((bf16[2,8,1024,128]{3,1,2,0:T(8,128)(2,1)}), bf16[2,8,2048,128]{3,1,2,0:T(8,128)(2,1)}) %all-gather.3.cloned.1.call-update) | async-done | bytes 8388624 | tf_op jit(solution)/shard_map/all_gather | solution.py:51
  310.7 5.9 slice_bitcast_fusion.13
  316.5 17.6 %fusion.2 = f32[8,1024,128]{2,1,0:T(8,128)} fusion(bf16[2,8,1024,2048]{3,2,1,0:T(8,128)(2,1)} %broadcast_multiply_fusion, bf16[8,2048,128]{2,0,1:T(8,128)(2,1)} %get-tuple-element.10), kind=kOutput, calls=%fused_computation.5 | convolution fusion | flops 4294967296 | bytes 41943040 | tf_op jit(solution)/shard_map/fmk,fkp->fmp/dot_general | solution.py:41
  334.1 17.6 %fusion.3 = f32[8,1024,128]{2,1,0:T(8,128)} fusion(bf16[2,8,1024,2048]{3,2,1,0:T(8,128)(2,1)} %broadcast_multiply_fusion, bf16[8,2048,128]{2,0,1:T(8,128)(2,1)} %get-tuple-element.9), kind=kOutput, calls=%fused_computation.6 | convolution fusion | flops 4294967296 | bytes 41943040 | tf_op jit(solution)/shard_map/fmk,fkp->fmp/dot_general | solution.py:35
  351.7 17.7 %fusion.39 = bf16[1,8,1024,128]{3,2,1,0:T(8,128)(2,1)S(1)} fusion(f32[8,1024,128]{2,1,0:T(8,128)} %fusion.2, bf16[8,2048,128]{2,0,1:T(8,128)(2,1)} %get-tuple-element.9, bf16[2,8,1024,2048]{3,2,1,0:T(8,128)(2,1)} %broadcast_multiply_fusion), kind=kOutput, calls=%fused_computation.58 | convolution fusion | flops 4297064448 | bytes 44040192 | tf_op jit(solution)/shard_map/fmk,fkp->fmp/dot_general | solution.py:44
  369.4 17.5 %fusion.38 = bf16[1,8,1024,128]{3,2,1,0:T(8,128)(2,1)} fusion(f32[8,1024,128]{2,1,0:T(8,128)} %fusion.3, bf16[8,2048,128]{2,0,1:T(8,128)(2,1)S(1)} %copy-done.6, bf16[2,8,1024,2048]{3,2,1,0:T(8,128)(2,1)} %broadcast_multiply_fusion), kind=kOutput, calls=%fused_computation.57 | convolution fusion | flops 4297064448 | bytes 44040192 | tf_op jit(solution)/shard_map/fmk,fkp->fmp/dot_general | solution.py:38
  391.6 98.8 %all_to_all.36 = bf16[2,8,1024,128]{3,1,0,2:T(8,128)(2,1)S(1)} all-to-all(bf16[2,8,1024,128]{3,1,0,2:T(8,128)(2,1)S(1)} %copy.41), channel_id=1, replica_groups=mesh['freq'=16,'rows'=2] {'freq'}, dimensions={2} | all-to-all | bytes 8388608 | tf_op jit(solution)/shard_map/all_to_all | solution.py:56
  491.6 17.6 %fusion.22 = f32[64,128,512,1]{2,1,3,0:T(8,128)} fusion(bf16[2,128,64,128]{3,2,1,0:T(8,128)(2,1)S(1)} %bitcast.85, f32[1,128,512]{2,1,0:T(8,128)S(1)} %copy-done.4, f32[1,128,512]{2,1,0:T(8,128)S(1)} %copy-done.2), kind=kOutput, calls=%fused_computation.41 | convolution fusion | flops 12885164032 | bytes 21495808 | tf_op jit(solution)/shard_map/kjrp,kjt->rpt/dot_general | solution.py:57
  509.2 18.9 %fusion.35 = bf16[2,128,64,128]{3,1,2,0:T(8,128)(2,1)S(1)} fusion(f32[64,128,512]{2,1,0:T(8,128)S(1)} %bitcast.84, f32[64,128,512,1]{2,1,3,0:T(8,128)} %fusion.22, s32[64,128]{1,0:T(8,128)S(1)} %copy-done.7, f32[1,128,512]{2,1,0:T(8,128)S(1)} %copy-done.4, f32[1,128,512]{2,1,0:T(8,128)S(1)} %copy-done.2), kind=kOutput, calls=%fused_computation.56 | convolution fusion | flops 12899844096 | bytes 38305792 | tf_op jit(solution)/shard_map/rpt,kjt->kjrp/dot_general | solution.py:64
  542.7 5.9 collective-permute-start.21
  553.1 30.6 %collective-permute-start.23 = (bf16[2,8,64,128]{3,1,2,0:T(8,128)(2,1)S(1)}, bf16[2,8,64,128]{3,1,2,0:T(8,128)(2,1)S(1)}, u32[]{:S(2)}, u32[]{:S(2)}) collective-permute-start(bf16[2,8,64,128]{3,1,2,0:T(8,128)(2,1)S(1)} %get-tuple-element.17), channel_id=1, source_target_pairs={{0,14},{2,16},{4,18},{6,20},{8,22},{10,24},{12,26},{14,28},{16,30}... | collective-permute-start | bytes 786440 | tf_op jit(solution)/shard_map/ppermute | solution.py:20
  583.9 28.3 %collective-permute-done.21 = bf16[2,8,64,128]{3,1,2,0:T(8,128)(2,1)S(1)} collective-permute-done((bf16[2,8,64,128]{3,1,2,0:T(8,128)(2,1)S(1)}, bf16[2,8,64,128]{3,1,2,0:T(8,128)(2,1)S(1)}, u32[]{:S(2)}, u32[]{:S(2)}) %collective-permute-start.21) | collective-permute-done | bytes 262176 | tf_op jit(solution)/shard_map/ppermute | solution.py:20
  614.2 5.1 collective-permute-done.26
  624.8 16.1 %fusion.17 = bf16[2,8,1024,128]{3,1,2,0:T(8,128)(2,1)} fusion(s32[]{:T(128)S(6)} %select_n.53, bf16[2,8,1024,128]{3,1,2,0:T(8,128)(2,1)S(1)} %slice_dynamic-update-slice_fusion), kind=kLoop, calls=%fused_computation.30 | loop fusion | flops 2097152 | bytes 8388612 | tf_op jit(solution)/shard_map/jit(_roll_dynamic)/concatenate | solution.py:22
  640.9 111.0 %all-gather.5.cloned.1.call-done = bf16[2,8,2048,128]{3,1,2,0:T(8,128)(2,1)} async-done(((bf16[2,8,1024,128]{3,1,2,0:T(8,128)(2,1)}), bf16[2,8,2048,128]{3,1,2,0:T(8,128)(2,1)}) %all-gather.5.cloned.1.call-update) | async-done | bytes 8388624 | tf_op jit(solution)/shard_map/all_gather | solution.py:51
  751.9 6.0 slice_bitcast_fusion.11
  757.9 17.6 %fusion = f32[8,1024,128]{2,1,0:T(8,128)} fusion(bf16[2,8,1024,2048]{3,2,1,0:T(8,128)(2,1)} %broadcast_multiply_fusion, bf16[8,2048,128]{2,0,1:T(8,128)(2,1)} %get-tuple-element.8), kind=kOutput, calls=%fused_computation.3 | convolution fusion | flops 4294967296 | bytes 41943040 | tf_op jit(solution)/shard_map/fmk,fkp->fmp/dot_general | solution.py:41
  775.4 18.0 %fusion.1 = f32[8,1024,128]{2,1,0:T(8,128)} fusion(bf16[2,8,1024,2048]{3,2,1,0:T(8,128)(2,1)} %broadcast_multiply_fusion, bf16[8,2048,128]{2,0,1:T(8,128)(2,1)} %get-tuple-element.6), kind=kOutput, calls=%fused_computation.4 | convolution fusion | flops 4294967296 | bytes 41943040 | tf_op jit(solution)/shard_map/fmk,fkp->fmp/dot_general | solution.py:35
  793.4 17.7 %fusion.41 = bf16[1,8,1024,128]{3,2,1,0:T(8,128)(2,1)S(1)} fusion(f32[8,1024,128]{2,1,0:T(8,128)} %fusion, bf16[8,2048,128]{2,0,1:T(8,128)(2,1)} %get-tuple-element.6, bf16[2,8,1024,2048]{3,2,1,0:T(8,128)(2,1)} %broadcast_multiply_fusion), kind=kOutput, calls=%fused_computation.60 | convolution fusion | flops 4297064448 | bytes 44040192 | tf_op jit(solution)/shard_map/fmk,fkp->fmp/dot_general | solution.py:44
  811.1 17.3 %fusion.40 = bf16[1,8,1024,128]{3,2,1,0:T(8,128)(2,1)} fusion(f32[8,1024,128]{2,1,0:T(8,128)} %fusion.1, bf16[8,2048,128]{2,0,1:T(8,128)(2,1)S(1)} %copy-done.5, bf16[2,8,1024,2048]{3,2,1,0:T(8,128)(2,1)} %broadcast_multiply_fusion), kind=kOutput, calls=%fused_computation.59 | convolution fusion | flops 4297064448 | bytes 44040192 | tf_op jit(solution)/shard_map/fmk,fkp->fmp/dot_general | solution.py:38
  833.1 98.8 %all_to_all.37 = bf16[2,8,1024,128]{3,1,0,2:T(8,128)(2,1)S(1)} all-to-all(bf16[2,8,1024,128]{3,1,0,2:T(8,128)(2,1)S(1)} %copy.49), channel_id=1, replica_groups=mesh['freq'=16,'rows'=2] {'freq'}, dimensions={2} | all-to-all | bytes 8388608 | tf_op jit(solution)/shard_map/all_to_all | solution.py:56
  933.0 20.1 %fusion.8 = f32[64,128,512]{2,1,0:T(8,128)} fusion(f32[64,128,512]{2,1,0:T(8,128)} %param.10, s32[64,128]{1,0:T(8,128)S(1)} %copy-done.7, bf16[2,128,64,128]{3,2,1,0:T(8,128)(2,1)S(1)} %bitcast.88, f32[1,128,512]{2,1,0:T(8,128)S(1)} %copy-done.4, f32[1,128,512]{2,1,0:T(8,128)S(1)} %copy-done.2), kind=kOutput, calls=%fused_computation.12 | convolution fusion | flops 12897746944 | bytes 38305792 | tf_op jit(solution)/shard_map/kjrp,kjt->rpt/dot_general | solution.py:57
  (128 shorter events, 66.7 us)
Async XLA Ops:
  6.5 304.1 %all-gather.3.cloned.1.call-start = ((), (), s32[]{:S(2)}) async-start(), calls=%async_computation.2 | async-start | bytes 12582912 | tf_op jit(solution)/shard_map/all_gather | solution.py:51
  30.9 77.7 %collective-permute-start = (bf16[2,8,64,128]{3,1,2,0:T(8,128)(2,1)}, bf16[2,8,64,128]{3,1,2,0:T(8,128)(2,1)}, u32[]{:S(2)}, u32[]{:S(2)}) collective-permute-start(bf16[2,8,64,128]{3,1,2,0:T(8,128)(2,1)} %get-tuple-element.40), channel_id=1, source_target_pairs={{0,30},{2,0},{4,2},{6,4},{8,6},{10,8},{12,10},{14,12},{16,14},{18,... | collective-permute-start | bytes 786440 | tf_op jit(solution)/shard_map/ppermute | solution.py:20
  31.0 81.3 %collective-permute-start.1 = (bf16[2,8,64,128]{3,1,2,0:T(8,128)(2,1)}, bf16[2,8,64,128]{3,1,2,0:T(8,128)(2,1)}, u32[]{:S(2)}, u32[]{:S(2)}) collective-permute-start(bf16[2,8,64,128]{3,1,2,0:T(8,128)(2,1)} %get-tuple-element.39), channel_id=1, source_target_pairs={{0,28},{2,30},{4,0},{6,2},{8,4},{10,6},{12,8},{14,10},{16,12},{18,... | collective-permute-start | bytes 786440 | tf_op jit(solution)/shard_map/ppermute | solution.py:20
  36.7 77.6 %collective-permute-start.2 = (bf16[2,8,64,128]{3,1,2,0:T(8,128)(2,1)S(1)}, bf16[2,8,64,128]{3,1,2,0:T(8,128)(2,1)}, u32[]{:S(2)}, u32[]{:S(2)}) collective-permute-start(bf16[2,8,64,128]{3,1,2,0:T(8,128)(2,1)S(1)} %get-tuple-element.38), channel_id=1, source_target_pairs={{0,26},{2,28},{4,30},{6,0},{8,2},{10,4},{12,6},{14,8},{16,10},{18,... | collective-permute-start | bytes 786440 | tf_op jit(solution)/shard_map/ppermute | solution.py:20
  37.9 81.1 %collective-permute-start.3 = (bf16[2,8,64,128]{3,1,2,0:T(8,128)(2,1)S(1)}, bf16[2,8,64,128]{3,1,2,0:T(8,128)(2,1)}, u32[]{:S(2)}, u32[]{:S(2)}) collective-permute-start(bf16[2,8,64,128]{3,1,2,0:T(8,128)(2,1)S(1)} %get-tuple-element.37), channel_id=1, source_target_pairs={{0,24},{2,26},{4,28},{6,30},{8,0},{10,2},{12,4},{14,6},{16,8},{18,... | collective-permute-start | bytes 786440 | tf_op jit(solution)/shard_map/ppermute | solution.py:20
  38.1 82.0 %collective-permute-start.4 = (bf16[2,8,64,128]{3,1,2,0:T(8,128)(2,1)S(1)}, bf16[2,8,64,128]{3,1,2,0:T(8,128)(2,1)}, u32[]{:S(2)}, u32[]{:S(2)}) collective-permute-start(bf16[2,8,64,128]{3,1,2,0:T(8,128)(2,1)S(1)} %get-tuple-element.36), channel_id=1, source_target_pairs={{0,22},{2,24},{4,26},{6,28},{8,30},{10,0},{12,2},{14,4},{16,6},{18... | collective-permute-start | bytes 786440 | tf_op jit(solution)/shard_map/ppermute | solution.py:20
  108.7 12.8 %collective-permute-start.5 = (bf16[2,8,64,128]{3,1,2,0:T(8,128)(2,1)S(1)}, bf16[2,8,64,128]{3,1,2,0:T(8,128)(2,1)S(1)}, u32[]{:S(2)}, u32[]{:S(2)}) collective-permute-start(bf16[2,8,64,128]{3,1,2,0:T(8,128)(2,1)S(1)} %get-tuple-element.35), channel_id=1, source_target_pairs={{0,20},{2,22},{4,24},{6,26},{8,28},{10,30},{12,0},{14,2},{16,4},{1... | collective-permute-start | bytes 786440 | tf_op jit(solution)/shard_map/ppermute | solution.py:20
  112.2 46.1 %collective-permute-start.6 = (bf16[2,8,64,128]{3,1,2,0:T(8,128)(2,1)S(1)}, bf16[2,8,64,128]{3,1,2,0:T(8,128)(2,1)S(1)}, u32[]{:S(2)}, u32[]{:S(2)}) collective-permute-start(bf16[2,8,64,128]{3,1,2,0:T(8,128)(2,1)S(1)} %get-tuple-element.34), channel_id=1, source_target_pairs={{0,18},{2,20},{4,22},{6,24},{8,26},{10,28},{12,30},{14,0},{16,2},{... | collective-permute-start | bytes 786440 | tf_op jit(solution)/shard_map/ppermute | solution.py:20
  114.4 53.3 %collective-permute-start.7 = (bf16[2,8,64,128]{3,1,2,0:T(8,128)(2,1)S(1)}, bf16[2,8,64,128]{3,1,2,0:T(8,128)(2,1)S(1)}, u32[]{:S(2)}, u32[]{:S(2)}) collective-permute-start(bf16[2,8,64,128]{3,1,2,0:T(8,128)(2,1)S(1)} %get-tuple-element.33), channel_id=1, source_target_pairs={{0,16},{2,18},{4,20},{6,22},{8,24},{10,26},{12,28},{14,30},{16,0},... | collective-permute-start | bytes 786440 | tf_op jit(solution)/shard_map/ppermute | solution.py:20
  119.1 50.7 %collective-permute-start.8 = (bf16[2,8,64,128]{3,1,2,0:T(8,128)(2,1)S(1)}, bf16[2,8,64,128]{3,1,2,0:T(8,128)(2,1)S(1)}, u32[]{:S(2)}, u32[]{:S(2)}) collective-permute-start(bf16[2,8,64,128]{3,1,2,0:T(8,128)(2,1)S(1)} %get-tuple-element.32), channel_id=1, source_target_pairs={{0,14},{2,16},{4,18},{6,20},{8,22},{10,24},{12,26},{14,28},{16,30}... | collective-permute-start | bytes 786440 | tf_op jit(solution)/shard_map/ppermute | solution.py:20
  120.1 62.8 %collective-permute-start.9 = (bf16[2,8,64,128]{3,1,2,0:T(8,128)(2,1)S(1)}, bf16[2,8,64,128]{3,1,2,0:T(8,128)(2,1)S(1)}, u32[]{:S(2)}, u32[]{:S(2)}) collective-permute-start(bf16[2,8,64,128]{3,1,2,0:T(8,128)(2,1)S(1)} %get-tuple-element.31), channel_id=1, source_target_pairs={{0,12},{2,14},{4,16},{6,18},{8,20},{10,22},{12,24},{14,26},{16,28}... | collective-permute-start | bytes 786440 | tf_op jit(solution)/shard_map/ppermute | solution.py:20
  121.5 61.7 %collective-permute-start.10 = (bf16[2,8,64,128]{3,1,2,0:T(8,128)(2,1)S(1)}, bf16[2,8,64,128]{3,1,2,0:T(8,128)(2,1)S(1)}, u32[]{:S(2)}, u32[]{:S(2)}) collective-permute-start(bf16[2,8,64,128]{3,1,2,0:T(8,128)(2,1)S(1)} %get-tuple-element.30), channel_id=1, source_target_pairs={{0,10},{2,12},{4,14},{6,16},{8,18},{10,20},{12,22},{14,24},{16,26}... | collective-permute-start | bytes 786440 | tf_op jit(solution)/shard_map/ppermute | solution.py:20
  158.3 24.9 %collective-permute-start.11 = (bf16[2,8,64,128]{3,1,2,0:T(8,128)(2,1)S(1)}, bf16[2,8,64,128]{3,1,2,0:T(8,128)(2,1)S(1)}, u32[]{:S(2)}, u32[]{:S(2)}) collective-permute-start(bf16[2,8,64,128]{3,1,2,0:T(8,128)(2,1)S(1)} %get-tuple-element.29), channel_id=1, source_target_pairs={{0,8},{2,10},{4,12},{6,14},{8,16},{10,18},{12,20},{14,22},{16,24},... | collective-permute-start | bytes 786440 | tf_op jit(solution)/shard_map/ppermute | solution.py:20
  167.6 15.7 %collective-permute-start.12 = (bf16[2,8,64,128]{3,1,2,0:T(8,128)(2,1)S(1)}, bf16[2,8,64,128]{3,1,2,0:T(8,128)(2,1)S(1)}, u32[]{:S(2)}, u32[]{:S(2)}) collective-permute-start(bf16[2,8,64,128]{3,1,2,0:T(8,128)(2,1)S(1)} %get-tuple-element.28), channel_id=1, source_target_pairs={{0,6},{2,8},{4,10},{6,12},{8,14},{10,16},{12,18},{14,20},{16,22},{... | collective-permute-start | bytes 786440 | tf_op jit(solution)/shard_map/ppermute | solution.py:20
  169.7 13.6 %collective-permute-start.13 = (bf16[2,8,64,128]{3,1,2,0:T(8,128)(2,1)S(1)}, bf16[2,8,64,128]{3,1,2,0:T(8,128)(2,1)S(1)}, u32[]{:S(2)}, u32[]{:S(2)}) collective-permute-start(bf16[2,8,64,128]{3,1,2,0:T(8,128)(2,1)S(1)} %get-tuple-element.27), channel_id=1, source_target_pairs={{0,4},{2,6},{4,8},{6,10},{8,12},{10,14},{12,16},{14,18},{16,20},{1... | collective-permute-start | bytes 786440 | tf_op jit(solution)/shard_map/ppermute | solution.py:20
  183.0 3.5 collective-permute-start.14
  203.4 548.5 %all-gather.5.cloned.1.call-start = ((), (), s32[]{:S(2)}) async-start(), calls=%async_computation.3 | async-start | bytes 12582912 | tf_op jit(solution)/shard_map/all_gather | solution.py:51
  531.5 8.9 collective-permute-start.15
  531.6 11.2 %collective-permute-start.16 = (bf16[2,8,64,128]{3,1,2,0:T(8,128)(2,1)S(1)}, bf16[2,8,64,128]{3,1,2,0:T(8,128)(2,1)S(1)}, u32[]{:S(2)}, u32[]{:S(2)}) collective-permute-start(bf16[2,8,64,128]{3,1,2,0:T(8,128)(2,1)S(1)} %get-tuple-element.24), channel_id=1, source_target_pairs={{0,28},{2,30},{4,0},{6,2},{8,4},{10,6},{12,8},{14,10},{16,12},{18,... | collective-permute-start | bytes 786440 | tf_op jit(solution)/shard_map/ppermute | solution.py:20
  534.8 17.6 %collective-permute-start.17 = (bf16[2,8,64,128]{3,1,2,0:T(8,128)(2,1)S(1)}, bf16[2,8,64,128]{3,1,2,0:T(8,128)(2,1)S(1)}, u32[]{:S(2)}, u32[]{:S(2)}) collective-permute-start(bf16[2,8,64,128]{3,1,2,0:T(8,128)(2,1)S(1)} %get-tuple-element.23), channel_id=1, source_target_pairs={{0,26},{2,28},{4,30},{6,0},{8,2},{10,4},{12,6},{14,8},{16,10},{18,... | collective-permute-start | bytes 786440 | tf_op jit(solution)/shard_map/ppermute | solution.py:20
  535.8 17.2 %collective-permute-start.18 = (bf16[2,8,64,128]{3,1,2,0:T(8,128)(2,1)S(1)}, bf16[2,8,64,128]{3,1,2,0:T(8,128)(2,1)S(1)}, u32[]{:S(2)}, u32[]{:S(2)}) collective-permute-start(bf16[2,8,64,128]{3,1,2,0:T(8,128)(2,1)S(1)} %get-tuple-element.22), channel_id=1, source_target_pairs={{0,24},{2,26},{4,28},{6,30},{8,0},{10,2},{12,4},{14,6},{16,8},{18,... | collective-permute-start | bytes 786440 | tf_op jit(solution)/shard_map/ppermute | solution.py:20
  537.5 46.2 %collective-permute-start.19 = (bf16[2,8,64,128]{3,1,2,0:T(8,128)(2,1)S(1)}, bf16[2,8,64,128]{3,1,2,0:T(8,128)(2,1)S(1)}, u32[]{:S(2)}, u32[]{:S(2)}) collective-permute-start(bf16[2,8,64,128]{3,1,2,0:T(8,128)(2,1)S(1)} %get-tuple-element.21), channel_id=1, source_target_pairs={{0,22},{2,24},{4,26},{6,28},{8,30},{10,0},{12,2},{14,4},{16,6},{18... | collective-permute-start | bytes 786440 | tf_op jit(solution)/shard_map/ppermute | solution.py:20
  540.4 43.4 %collective-permute-start.20 = (bf16[2,8,64,128]{3,1,2,0:T(8,128)(2,1)S(1)}, bf16[2,8,64,128]{3,1,2,0:T(8,128)(2,1)S(1)}, u32[]{:S(2)}, u32[]{:S(2)}) collective-permute-start(bf16[2,8,64,128]{3,1,2,0:T(8,128)(2,1)S(1)} %get-tuple-element.20), channel_id=1, source_target_pairs={{0,20},{2,22},{4,24},{6,26},{8,28},{10,30},{12,0},{14,2},{16,4},{1... | collective-permute-start | bytes 786440 | tf_op jit(solution)/shard_map/ppermute | solution.py:20
  542.7 69.5 %collective-permute-start.21 = (bf16[2,8,64,128]{3,1,2,0:T(8,128)(2,1)S(1)}, bf16[2,8,64,128]{3,1,2,0:T(8,128)(2,1)S(1)}, u32[]{:S(2)}, u32[]{:S(2)}) collective-permute-start(bf16[2,8,64,128]{3,1,2,0:T(8,128)(2,1)S(1)} %get-tuple-element.19), channel_id=1, source_target_pairs={{0,18},{2,20},{4,22},{6,24},{8,26},{10,28},{12,30},{14,0},{16,2},{... | collective-permute-start | bytes 786440 | tf_op jit(solution)/shard_map/ppermute | solution.py:20
  552.4 59.9 %collective-permute-start.22 = (bf16[2,8,64,128]{3,1,2,0:T(8,128)(2,1)S(1)}, bf16[2,8,64,128]{3,1,2,0:T(8,128)(2,1)S(1)}, u32[]{:S(2)}, u32[]{:S(2)}) collective-permute-start(bf16[2,8,64,128]{3,1,2,0:T(8,128)(2,1)S(1)} %get-tuple-element.18), channel_id=1, source_target_pairs={{0,16},{2,18},{4,20},{6,22},{8,24},{10,26},{12,28},{14,30},{16,0},... | collective-permute-start | bytes 786440 | tf_op jit(solution)/shard_map/ppermute | solution.py:20
  553.1 59.4 %collective-permute-start.23 = (bf16[2,8,64,128]{3,1,2,0:T(8,128)(2,1)S(1)}, bf16[2,8,64,128]{3,1,2,0:T(8,128)(2,1)S(1)}, u32[]{:S(2)}, u32[]{:S(2)}) collective-permute-start(bf16[2,8,64,128]{3,1,2,0:T(8,128)(2,1)S(1)} %get-tuple-element.17), channel_id=1, source_target_pairs={{0,14},{2,16},{4,18},{6,20},{8,22},{10,24},{12,26},{14,28},{16,30}... | collective-permute-start | bytes 786440 | tf_op jit(solution)/shard_map/ppermute | solution.py:20
  583.7 28.9 %collective-permute-start.24 = (bf16[2,8,64,128]{3,1,2,0:T(8,128)(2,1)S(1)}, bf16[2,8,64,128]{3,1,2,0:T(8,128)(2,1)S(1)}, u32[]{:S(2)}, u32[]{:S(2)}) collective-permute-start(bf16[2,8,64,128]{3,1,2,0:T(8,128)(2,1)S(1)} %get-tuple-element.16), channel_id=1, source_target_pairs={{0,12},{2,14},{4,16},{6,18},{8,20},{10,22},{12,24},{14,26},{16,28}... | collective-permute-start | bytes 786440 | tf_op jit(solution)/shard_map/ppermute | solution.py:20
  583.8 30.3 %collective-permute-start.25 = (bf16[2,8,64,128]{3,1,2,0:T(8,128)(2,1)S(1)}, bf16[2,8,64,128]{3,1,2,0:T(8,128)(2,1)S(1)}, u32[]{:S(2)}, u32[]{:S(2)}) collective-permute-start(bf16[2,8,64,128]{3,1,2,0:T(8,128)(2,1)S(1)} %get-tuple-element.15), channel_id=1, source_target_pairs={{0,10},{2,12},{4,14},{6,16},{8,18},{10,20},{12,22},{14,24},{16,26}... | collective-permute-start | bytes 786440 | tf_op jit(solution)/shard_map/ppermute | solution.py:20
  612.2 7.1 collective-permute-start.26
  612.3 11.2 %collective-permute-start.27 = (bf16[2,8,64,128]{3,1,2,0:T(8,128)(2,1)S(1)}, bf16[2,8,64,128]{3,1,2,0:T(8,128)(2,1)S(1)}, u32[]{:S(2)}, u32[]{:S(2)}) collective-permute-start(bf16[2,8,64,128]{3,1,2,0:T(8,128)(2,1)S(1)} %get-tuple-element.13), channel_id=1, source_target_pairs={{0,6},{2,8},{4,10},{6,12},{8,14},{10,16},{12,18},{14,20},{16,22},{... | collective-permute-start | bytes 786440 | tf_op jit(solution)/shard_map/ppermute | solution.py:20
  612.5 11.0 %collective-permute-start.28 = (bf16[2,8,64,128]{3,1,2,0:T(8,128)(2,1)S(1)}, bf16[2,8,64,128]{3,1,2,0:T(8,128)(2,1)S(1)}, u32[]{:S(2)}, u32[]{:S(2)}) collective-permute-start(bf16[2,8,64,128]{3,1,2,0:T(8,128)(2,1)S(1)} %get-tuple-element.12), channel_id=1, source_target_pairs={{0,4},{2,6},{4,8},{6,10},{8,12},{10,14},{12,16},{14,18},{16,20},{1... | collective-permute-start | bytes 786440 | tf_op jit(solution)/shard_map/ppermute | solution.py:20
  612.6 12.1 %collective-permute-start.29 = (bf16[2,8,64,128]{3,1,2,0:T(8,128)(2,1)S(1)}, bf16[2,8,64,128]{3,1,2,0:T(8,128)(2,1)S(1)}, u32[]{:S(2)}, u32[]{:S(2)}) collective-permute-start(bf16[2,8,64,128]{3,1,2,0:T(8,128)(2,1)S(1)} %get-tuple-element.11), channel_id=1, source_target_pairs={{0,2},{2,4},{4,6},{6,8},{8,10},{10,12},{12,14},{14,16},{16,18},{18... | collective-permute-start | bytes 786440 | tf_op jit(solution)/shard_map/ppermute | solution.py:20
  (13 other events, 172.3 us)
Sparse Core Ops, SparseCore 0:
  203.5 107.0 all-gather.2
  641.1 110.7 all-gather.4
